TPU v7x, 32 devices: a whole 2x2x4 slice. The times are simulated.
32 devices in a mesh: dp: 4 (over z), adapter: 2 (over x), fsdp: 4 (over y, core).
Axes of the slice: x: 2, y: 2, z: 4, core: 2. Of those that a mesh axis runs over, the one named last changes fastest.
Arguments:
- adapter_index: int32 [768], P(('dp', 'adapter', 'fsdp')), may hold values from 0 to 1, as said below
- output_gradient: bfloat16 [768, 4096], P(('dp', 'adapter', 'fsdp')), may hold values from -6 to 6
- hidden: bfloat16 [768, 14336], P(('dp', 'adapter', 'fsdp')), may hold values from -6 to 6
- frozen_down_weight: bfloat16 [14336, 4096], P('adapter', 'fsdp'), may hold values from -0.046875 to 0.046875
- adapter_input_maps: bfloat16 [2, 16, 14336], P('adapter'), may hold values from -0.046875 to 0.046875
- adapter_output_maps: bfloat16 [2, 16, 4096], P('adapter'), may hold values from -1.5 to 1.5
Outputs:
- hidden_gradient: bfloat16 [768, 14336], P(('dp', 'adapter', 'fsdp'))
- adapter_input_gradient: float32 [2, 16, 14336], P('adapter')
- adapter_output_gradient: float32 [2, 16, 4096], P('adapter')
Inputs may be any that keep to these rules, and one draw needn't show every extreme that they name: `adapter_index`: adapter i sits at index i // 1 of adapter. Of the 24 tokens of one device (aligned blocks of 24 rows), at most 12 name adapters at the same index; in every draw one index is named by exactly 12 tokens of every device.
All inputs are finite; a program needn't handle non-finite values.
Results may differ from a plain program's by a relative error of at most 0.015.
Values may be sent and summed in bfloat16 or wider, within the bound.
A program may use at most 64 MiB of HBM per device.

v0:
```python
import jax
import jax.numpy as jnp
from jax import lax
from jax.sharding import PartitionSpec as P

adapter_scale = 2.0


def on_device(
    adapter_index,
    output_gradient,
    hidden,
    frozen_down_weight,
    adapter_input_maps,
    adapter_output_maps,
):
    tok_rows = output_gradient.shape[0]
    token_tenants = lax.axis_size("adapter")
    fibres = lax.axis_size("fsdp")
    groups = lax.axis_size("dp")
    tenant_token_count = adapter_input_maps.shape[0]
    adapter_rank_size = adapter_input_maps.shape[1]
    hidden_units_width = hidden.shape[1]
    model_dimension_width = output_gradient.shape[1]
    capacity = max(2, min(tok_rows // 2, 2 * tok_rows // token_tenants))
    every_token = tok_rows * token_tenants * fibres * groups
    scaling_factor = adapter_scale * (tenant_token_count * token_tenants) / every_token
    slab_width = frozen_down_weight.shape[1]
    own_columns = lax.all_to_all(output_gradient, "fsdp", split_axis=1, concat_axis=0, tiled=True)
    spread = lax.all_gather(own_columns, "adapter", axis=0, tiled=True)
    blocks = spread.reshape(token_tenants, fibres, tok_rows, slab_width)
    per_fibre = token_tenants * tok_rows
    taken = blocks
    taken = jnp.transpose(taken, (1, 0, 2, 3)).reshape(
        per_fibre * lax.axis_size("fsdp"), slab_width
    )
    partial_base = lax.psum_scatter(
        lax.dot_general(
            taken, frozen_down_weight, (((1,), (1,)), ((), ())), preferred_element_type=jnp.float32
        ).astype(jnp.bfloat16),
        "fsdp",
        scatter_dimension=0,
        tiled=True,
    )
    frozen_term = lax.all_to_all(partial_base, "adapter", split_axis=0, concat_axis=1, tiled=True)
    owner_of = adapter_index // tenant_token_count
    local_of = adapter_index - owner_of * tenant_token_count
    same_owner = owner_of[:, None] == owner_of[None, :]
    earlier = jnp.arange(tok_rows)[None, :] < jnp.arange(tok_rows)[:, None]
    position = jnp.sum((same_owner & earlier).astype(jnp.int32), axis=1)
    slot_of = owner_of * capacity + position
    slot_count = token_tenants * capacity
    placing = (jnp.arange(slot_count, dtype=jnp.int32)[:, None] == slot_of[None, :]).astype(
        jnp.bfloat16
    )
    send_out = jnp.dot(placing, output_gradient, preferred_element_type=jnp.float32).astype(
        jnp.bfloat16
    )
    send_hidden = jnp.dot(placing, hidden, preferred_element_type=jnp.float32).astype(jnp.bfloat16)
    send_tag = jnp.dot(
        placing, (local_of + 1).astype(jnp.bfloat16), preferred_element_type=jnp.float32
    ).astype(jnp.bfloat16)
    recv_out, recv_hidden, recv_tag = (
        lax.all_to_all(send_out, "adapter", split_axis=0, concat_axis=0, tiled=True),
        lax.all_to_all(send_hidden, "adapter", split_axis=0, concat_axis=0, tiled=True),
        lax.all_to_all(send_tag, "adapter", split_axis=0, concat_axis=0, tiled=True),
    )
    flattened_input_map = adapter_input_maps.reshape(
        tenant_token_count * adapter_rank_size, hidden_units_width
    )
    flattened_output_map = adapter_output_maps.reshape(
        tenant_token_count * adapter_rank_size, model_dimension_width
    )
    chosen = (
        recv_tag.astype(jnp.float32)[:, None]
        == (jnp.arange(tenant_token_count) + 1).astype(jnp.float32)[None, :]
    )
    row_mask = jnp.repeat(chosen, adapter_rank_size, axis=1).astype(jnp.float32)
    multiplier = (
        lax.dot_general(
            recv_out,
            flattened_output_map,
            (((1,), (1,)), ((), ())),
            preferred_element_type=jnp.float32,
        )
        * row_mask
    ).astype(jnp.bfloat16)
    low_rank = (
        lax.dot_general(
            recv_hidden,
            flattened_input_map,
            (((1,), (1,)), ((), ())),
            preferred_element_type=jnp.float32,
        )
        * row_mask
    ).astype(jnp.bfloat16)
    adapter_token_rows = (
        adapter_scale * jnp.dot(multiplier, flattened_input_map, preferred_element_type=jnp.float32)
    ).astype(jnp.bfloat16)
    grad_a_part = lax.dot_general(
        multiplier, recv_hidden, (((0,), (0,)), ((), ())), preferred_element_type=jnp.float32
    )
    grad_b_part = lax.dot_general(
        low_rank, recv_out, (((0,), (0,)), ((), ())), preferred_element_type=jnp.float32
    )
    backward_result = lax.all_to_all(
        adapter_token_rows, "adapter", split_axis=0, concat_axis=0, tiled=True
    )
    adapter_selection = lax.dot_general(
        placing, backward_result, (((0,), (0,)), ((), ())), preferred_element_type=jnp.float32
    )
    hidden_gradient = (frozen_term.astype(jnp.float32) + adapter_selection).astype(jnp.bfloat16)
    input_map_total, output_map_total = (
        lax.psum(grad_a_part.astype(jnp.bfloat16), ("dp", "fsdp")).astype(jnp.float32),
        lax.psum(grad_b_part.astype(jnp.bfloat16), ("dp", "fsdp")).astype(jnp.float32),
    )
    adapter_input_gradient = (scaling_factor * input_map_total).reshape(
        tenant_token_count, adapter_rank_size, hidden_units_width
    )
    adapter_output_gradient = (scaling_factor * output_map_total).reshape(
        tenant_token_count, adapter_rank_size, model_dimension_width
    )
    return (hidden_gradient, adapter_input_gradient, adapter_output_gradient)


def solution(mesh):
    in_specs = (
        P(("dp", "adapter", "fsdp")),
        P(("dp", "adapter", "fsdp"), None),
        P(("dp", "adapter", "fsdp"), None),
        P("adapter", "fsdp"),
        P("adapter", None, None),
        P("adapter", None, None),
    )
    out_specs = (
        P(("dp", "adapter", "fsdp"), None),
        P("adapter", None, None),
        P("adapter", None, None),
    )
    return jax.shard_map(
        on_device, mesh=mesh, in_specs=in_specs, out_specs=out_specs, check_vma=False
    )
```

profile of v0, /device:TPU:0, one launch (start us, length us, event | category | flops | bytes accessed | tf_op | source)
XLA Modules:
  0.0 185.1 jit_solution(1483464234489830159)
XLA Ops:
  8.0 0.0 copy-start
  8.0 0.0 copy-start.2
  8.0 0.9 convert_reduce_fusion
  9.0 0.7 multiply_add_fusion
  9.6 0.1 fusion.4
  9.8 0.7 all_to_all.71
  10.4 4.2 %all-to-all-start.2 = ((bf16[2,12,1]{1,2,0:T(2,128)(2,1)}), bf16[2,12,1]{1,2,0:T(2,128)(2,1)S(1)}, u32[]{:S(2)}, u32[]{:S(2)}) async-start(bf16[2,12,1]{1,2,0:T(2,128)(2,1)} %all_to_all.71), calls=%async_computation.3 | async-start | bytes 2048 | tf_op jit(solution)/shard_map/all_to_all | solution.py:66
  14.6 1.1 convolution_convert_fusion.3
  15.8 0.8 all_to_all.62
  16.5 1.8 all-to-all-done.2
  18.3 3.4 %all-to-all-start.3 = ((bf16[2,12,4096]{2,1,0:T(8,128)(2,1)}), bf16[2,12,4096]{2,1,0:T(8,128)(2,1)S(1)}, u32[]{:S(2)}, u32[]{:S(2)}) async-start(bf16[2,12,4096]{2,1,0:T(8,128)(2,1)} %all_to_all.62), calls=%async_computation.4 | async-start | bytes 524288 | tf_op jit(solution)/shard_map/all_to_all | solution.py:64
  21.8 0.0 copy-done.2
  21.8 0.7 copy.30
  22.5 4.5 %all-to-all-done.3 = bf16[2,12,4096]{2,1,0:T(8,128)(2,1)S(1)} async-done(((bf16[2,12,4096]{2,1,0:T(8,128)(2,1)}), bf16[2,12,4096]{2,1,0:T(8,128)(2,1)S(1)}, u32[]{:S(2)}, u32[]{:S(2)}) %all-to-all-start.3) | async-done | bytes 196640 | tf_op jit(solution)/shard_map/all_to_all | solution.py:64
  27.0 3.4 %all-to-all-start = ((bf16[24,4,1024]{2,0,1:T(8,128)(2,1)}), bf16[24,4,1024]{2,0,1:T(8,128)(2,1)S(1)}, u32[]{:S(2)}, u32[]{:S(2)}) async-start(bf16[24,4,1024]{2,0,1:T(8,128)(2,1)} %bitcast.43), calls=%async_computation | async-start | bytes 393216 | tf_op jit(solution)/shard_map/all_to_all | solution.py:29
  30.3 0.0 copy-done
  30.3 0.3 convolution_convert_fusion
  30.7 1.1 all_to_all.68
  31.8 0.0 copy-start.4
  31.8 3.8 %all-to-all-done = bf16[24,4,1024]{2,0,1:T(8,128)(2,1)S(1)} async-done(((bf16[24,4,1024]{2,0,1:T(8,128)(2,1)}), bf16[24,4,1024]{2,0,1:T(8,128)(2,1)S(1)}, u32[]{:S(2)}, u32[]{:S(2)}) %all-to-all-start) | async-done | bytes 196640 | tf_op jit(solution)/shard_map/all_to_all | solution.py:29
  35.6 3.6 %all-to-all-start.5 = ((bf16[2,12,14336]{2,1,0:T(8,128)(2,1)}), bf16[2,12,14336]{2,1,0:T(8,128)(2,1)S(1)}, u32[]{:S(2)}, u32[]{:S(2)}) async-start(bf16[2,12,14336]{2,1,0:T(8,128)(2,1)} %all_to_all.68), calls=%async_computation.6 | async-start | bytes 1835008 | tf_op jit(solution)/shard_map/all_to_all | solution.py:65
  39.2 0.0 all-reduce.3.cloned.1.call-start
  39.2 0.1 eq.45
  39.3 0.1 all_to_all.64
  39.4 0.0 copy-done.4
  39.4 0.2 fusion.2
  39.6 15.7 %all_gather.3 = bf16[192,1024]{1,0:T(8,128)(2,1)S(1)} all-gather(bf16[96,1024]{1,0:T(8,128)(2,1)S(1)} %bitcast.47), channel_id=1, replica_groups=mesh['dp'=4,'adapter'=2,'fsdp'=4] {'adapter'}, dimensions={0}, use_global_device_ids=true | all-gather | bytes 589824 | tf_op jit(solution)/shard_map/all_gather | solution.py:30
  55.3 0.0 copy-start.1
  55.3 0.0 all-to-all-done.5
  55.3 0.2 all_to_all.70
  55.5 1.1 convolution_convert_fusion.1
  56.6 0.0 copy-done.1
  56.6 1.2 convolution_convert_fusion.4
  57.8 0.0 all-reduce.3.cloned.1.call-update
  57.8 0.0 reduce-scatter.2.cloned.1.call-start
  57.9 11.7 %convolution_convert_fusion.2 = bf16[192,7168]{1,0:T(8,128)(2,1)} fusion(bf16[192,1024]{1,0:T(8,128)(2,1)S(1)} %bitcast.49, bf16[7168,1024]{1,0:T(8,128)(2,1)} %param.9), kind=kOutput, calls=%fused_computation.6 | convolution fusion | flops 2819948544 | bytes 17825792 | tf_op jit(solution)/shard_map/dot_general | solution.py:38
  69.6 0.0 reduce-scatter.2.cloned.1.call-update
  69.6 0.4 fusion
  70.0 0.2 all_to_all.65
  70.2 13.5 %all_to_all.78 = bf16[2,12,14336]{2,1,0:T(8,128)(2,1)S(1)} all-to-all(bf16[2,12,14336]{2,1,0:T(8,128)(2,1)S(1)} %all_to_all.65), channel_id=1, replica_groups=mesh['dp'=4,'adapter'=2,'fsdp'=4] {'adapter'}, dimensions={0} | all-to-all | bytes 1376256 | tf_op jit(solution)/shard_map/all_to_all | solution.py:106
  83.7 0.2 all_to_all.67
  83.9 77.5 %all-reduce.3.cloned.1.call-done = (bf16[16,14336]{1,0:T(8,128)(2,1)}, bf16[16,4096]{1,0:T(8,128)(2,1)}) async-done(((bf16[16,14336]{1,0:T(8,128)(2,1)}, bf16[16,4096]{1,0:T(8,128)(2,1)}), (bf16[16,14336]{1,0:T(8,128)(2,1)}, bf16[16,4096]{1,0:T(8,128)(2,1)})) %all-reduce.3.cloned.1.call-update) | async-done | bytes 589840 | tf_op jit(solution)/shard_map/psum | solution.py:114
  161.4 0.0 copy-start.3
  161.4 2.0 %multiply_bitcast_fusion = f32[1,16,14336]{2,1,0:T(8,128)} fusion(bf16[16,14336]{1,0:T(8,128)(2,1)} %get-tuple-element.3), kind=kLoop, calls=%fused_computation.16 | loop fusion | flops 458752 | bytes 1376256 | tf_op jit(solution)/shard_map/reshape | solution.py:117
  163.4 0.0 reduce-scatter.2.cloned.1.call-done
  163.4 3.5 %all-to-all-start.1 = ((bf16[2,24,7168]{2,1,0:T(8,128)(2,1)}), bf16[2,24,7168]{2,1,0:T(8,128)(2,1)S(1)}, u32[]{:S(2)}, u32[]{:S(2)}) async-start(bf16[2,24,7168]{2,1,0:T(8,128)(2,1)} %bitcast.48), calls=%async_computation.2 | async-start | bytes 1376256 | tf_op jit(solution)/shard_map/all_to_all | solution.py:45
  166.9 0.0 copy-done.3
  167.0 0.7 multiply_bitcast_fusion.1
  167.7 8.5 %all-to-all-done.1 = bf16[2,24,7168]{2,1,0:T(8,128)(2,1)S(1)} async-done(((bf16[2,24,7168]{2,1,0:T(8,128)(2,1)}), bf16[2,24,7168]{2,1,0:T(8,128)(2,1)S(1)}, u32[]{:S(2)}, u32[]{:S(2)}) %all-to-all-start.1) | async-done | bytes 688160 | tf_op jit(solution)/shard_map/all_to_all | solution.py:45
  176.2 0.1 convert_bitcast_fusion
  176.3 0.1 copy.28
  176.4 1.2 fusion.1
  (2 shorter events, 0.0 us)
Async XLA Ops:
  8.0 22.3 %copy-start = (bf16[24,14336]{1,0:T(8,128)(2,1)S(1)}, bf16[24,14336]{1,0:T(8,128)(2,1)}, u32[]{:S(2)}) copy-start(bf16[24,14336]{1,0:T(8,128)(2,1)} %param.8) | copy-start | bytes 2064388
  8.0 13.8 %copy-start.2 = (bf16[24,4096]{1,0:T(8,128)(2,1)S(1)}, bf16[24,4096]{1,0:T(8,128)(2,1)}, u32[]{:S(2)}) copy-start(bf16[24,4096]{1,0:T(8,128)(2,1)} %param.7) | copy-start | bytes 589828
  10.4 7.9 %all-to-all-start.2 = ((bf16[2,12,1]{1,2,0:T(2,128)(2,1)}), bf16[2,12,1]{1,2,0:T(2,128)(2,1)S(1)}, u32[]{:S(2)}, u32[]{:S(2)}) async-start(bf16[2,12,1]{1,2,0:T(2,128)(2,1)} %all_to_all.71), calls=%async_computation.3 | async-start | bytes 2048 | tf_op jit(solution)/shard_map/all_to_all | solution.py:66
  18.3 8.6 %all-to-all-start.3 = ((bf16[2,12,4096]{2,1,0:T(8,128)(2,1)}), bf16[2,12,4096]{2,1,0:T(8,128)(2,1)S(1)}, u32[]{:S(2)}, u32[]{:S(2)}) async-start(bf16[2,12,4096]{2,1,0:T(8,128)(2,1)} %all_to_all.62), calls=%async_computation.4 | async-start | bytes 524288 | tf_op jit(solution)/shard_map/all_to_all | solution.py:64
  27.0 8.6 %all-to-all-start = ((bf16[24,4,1024]{2,0,1:T(8,128)(2,1)}), bf16[24,4,1024]{2,0,1:T(8,128)(2,1)S(1)}, u32[]{:S(2)}, u32[]{:S(2)}) async-start(bf16[24,4,1024]{2,0,1:T(8,128)(2,1)} %bitcast.43), calls=%async_computation | async-start | bytes 393216 | tf_op jit(solution)/shard_map/all_to_all | solution.py:29
  31.8 7.6 %copy-start.4 = (bf16[1,16,4096]{2,1,0:T(8,128)(2,1)S(1)}, bf16[1,16,4096]{2,1,0:T(8,128)(2,1)}, u32[]{:S(2)}) copy-start(bf16[1,16,4096]{2,1,0:T(8,128)(2,1)} %param.11) | copy-start | bytes 393220
  35.6 19.7 %all-to-all-start.5 = ((bf16[2,12,14336]{2,1,0:T(8,128)(2,1)}), bf16[2,12,14336]{2,1,0:T(8,128)(2,1)S(1)}, u32[]{:S(2)}, u32[]{:S(2)}) async-start(bf16[2,12,14336]{2,1,0:T(8,128)(2,1)} %all_to_all.68), calls=%async_computation.6 | async-start | bytes 1835008 | tf_op jit(solution)/shard_map/all_to_all | solution.py:65
  39.2 122.2 %all-reduce.3.cloned.1.call-start = ((), (), s32[]{:S(2)}) async-start(), calls=%async_computation.8 | async-start | bytes 1179648 | tf_op jit(solution)/shard_map/psum | solution.py:114
  55.3 1.3 copy-start.1
  57.8 105.6 %reduce-scatter.2.cloned.1.call-start = ((), (), s32[]{:S(2)}) async-start(), calls=%async_computation.7 | async-start | bytes 3440640 | tf_op jit(solution)/shard_map/reduce_scatter | solution.py:37
  161.4 5.6 %copy-start.3 = (bf16[16,4096]{1,0:T(8,128)(2,1)S(1)}, bf16[16,4096]{1,0:T(8,128)(2,1)}, u32[]{:S(2)}) copy-start(bf16[16,4096]{1,0:T(8,128)(2,1)} %get-tuple-element.4) | copy-start | bytes 393220
  163.4 12.8 %all-to-all-start.1 = ((bf16[2,24,7168]{2,1,0:T(8,128)(2,1)}), bf16[2,24,7168]{2,1,0:T(8,128)(2,1)S(1)}, u32[]{:S(2)}, u32[]{:S(2)}) async-start(bf16[2,24,7168]{2,1,0:T(8,128)(2,1)} %bitcast.48), calls=%async_computation.2 | async-start | bytes 1376256 | tf_op jit(solution)/shard_map/all_to_all | solution.py:45
Sparse Core Ops, SparseCore 0:
  58.0 103.3 all-reduce.2
Sparse Core Ops, SparseCore 1:
  69.7 35.7 reduce-scatter.1
where the time goes:
time: 186 us; the launch traced here: 185 us
  waiting for transfers between devices  96.1 us (52%)
  blocking collectives  29.2 us (16%)
  starting transfers between devices  18.2 us (10%)
  matrix products  17.3 us (9%)
  between operations  15.6 us (8%)
  other arithmetic  4.49 us (2%)
  local copies, waits for them, and re-layouts  4.02 us (2%)
    psum x1, waiting for transfers between devices, on_device(): lax.psum(grad_a_part.astype(jnp.bfloat16), ('dp', 'fsdp'))  77.5 us
    all_gather x1, blocking collectives, on_device(): spread = lax.all_gather(own_columns, 'adapter', axis=0, tiled=True)  15.7 us
    all_to_all x1, blocking collectives, on_device(): lax.all_to_all(adapter_token_rows, 'adapter', split_axis=0, concat_axis=0...  13.5 us
    dot_general x1, matrix products, on_device(): lax.dot_general(taken, frozen_down_weight, (((1,), (1,)), ((), ())), pref...  11.7 us
    all_to_all x1, waiting for transfers between devices, on_device(): lax.all_to_all(partial_base, 'adapter', split_axis=0, concat_axis=1, tile...  8.49 us
    all_to_all x1, waiting for transfers between devices, on_device(): lax.all_to_all(send_out, 'adapter', split_axis=0, concat_axis=0, tiled=True)  4.46 us
    all_to_all x1, starting transfers between devices, on_device(): lax.all_to_all(send_tag, 'adapter', split_axis=0, concat_axis=0, tiled=True)  4.23 us
    all_to_all x1, waiting for transfers between devices, on_device(): lax.all_to_all(output_gradient, 'fsdp', split_axis=1, concat_axis=0, tile...  3.82 us
  transfers between devices with their start and end apart: 7, of which 5 were waited for; matrix products, arithmetic and copies ran while one was open for 9% of the time, Pallas kernels for 0%

commit v1 on v0

--- a/solution.py
+++ b/solution.py
@@ -111,7 +111,7 @@
     )
     hidden_gradient = (frozen_term.astype(jnp.float32) + adapter_selection).astype(jnp.bfloat16)
     input_map_total, output_map_total = (
-        lax.psum(grad_a_part.astype(jnp.bfloat16), ("dp", "fsdp")).astype(jnp.float32),
+        lax.psum(lax.psum(grad_a_part.astype(jnp.bfloat16), "fsdp"), "dp").astype(jnp.float32),
         lax.psum(grad_b_part.astype(jnp.bfloat16), ("dp", "fsdp")).astype(jnp.float32),
     )
     adapter_input_gradient = (scaling_factor * input_map_total).reshape(

time: 186 us -> 271 us (1.46)
  waiting for transfers between devices: 96.1 us -> 192 us
  blocking collectives: 29.2 us -> 15.7 us
  starting transfers between devices: 18.2 us -> 21.8 us
    psum x1 -> x3, waiting for transfers between devices: 77.5 us -> 144 us  [the longest x1 92.2 us: on_device(): lax.psum(grad_b_part.astype(jnp.bfloat16), ('dp', 'fsdp'))]
    reduce_scatter x1, waiting for transfers between devices: 0.01 us -> 37.7 us  [on_device(): lax.psum_scatter(lax.dot_general(taken, frozen_down_weight, (((1,), (1,))...]
    all_to_all x1 -> x0, blocking collectives: 13.5 us -> none  [on_device(): lax.all_to_all(adapter_token_rows, 'adapter', split_axis=0, concat_axis=0...]
    all_to_all x1, waiting for transfers between devices: 8.49 us -> 0.01 us  [on_device(): lax.all_to_all(partial_base, 'adapter', split_axis=0, concat_axis=1, tile...]
    all_to_all x0 -> x1, starting transfers between devices: none -> 3.56 us  [on_device(): lax.all_to_all(adapter_token_rows, 'adapter', split_axis=0, concat_axis=0...]
  transfers between devices with their start and end apart: 7 -> 10, of which waited for: 5 -> 7; matrix products, arithmetic and copies ran while one was open for 9% -> 7% of each run, Pallas kernels for 0% -> 0%
where the time goes in v1:
time: 271 us
  waiting for transfers between devices  192 us (71%)
  starting transfers between devices  21.8 us (8%)
  matrix products  17.4 us (6%)
  blocking collectives  15.7 us (6%)
  between operations  13.9 us (5%)
  other arithmetic  5.36 us (2%)
  local copies, waits for them, and re-layouts  4.94 us (2%)
    psum x1, waiting for transfers between devices, on_device(): lax.psum(grad_b_part.astype(jnp.bfloat16), ('dp', 'fsdp'))  92.2 us
    reduce_scatter x1, waiting for transfers between devices, on_device(): lax.psum_scatter(lax.dot_general(taken, frozen_down_weight, (((1,), (1,))...  37.7 us
    psum x1, waiting for transfers between devices, on_device(): lax.psum(lax.psum(grad_a_part.astype(jnp.bfloat16), 'fsdp'), 'dp')  36.3 us
    all_gather x1, blocking collectives, on_device(): spread = lax.all_gather(own_columns, 'adapter', axis=0, tiled=True)  15.7 us
    psum x1, waiting for transfers between devices, on_device(): lax.psum(grad_a_part.astype(jnp.bfloat16), 'fsdp')  15.2 us
    dot_general x1, matrix products, on_device(): lax.dot_general(taken, frozen_down_weight, (((1,), (1,)), ((), ())), pref...  11.8 us
  transfers between devices with their start and end apart: 10, of which 7 were waited for; matrix products, arithmetic and copies ran while one was open for 7% of the time, Pallas kernels for 0%

profile of v1, /device:TPU:0, one launch (start us, length us, event | category | flops | bytes accessed | tf_op | source)
XLA Modules:
  0.0 270.7 jit_solution(2769618833912638409)
XLA Ops:
  7.2 0.0 copy-start
  7.2 0.0 copy-start.2
  7.2 0.9 convert_reduce_fusion
  8.1 0.7 multiply_add_fusion
  8.8 0.1 fusion.4
  8.9 0.7 all_to_all.71
  9.6 4.2 %all-to-all-start.2 = ((bf16[2,12,1]{1,2,0:T(2,128)(2,1)}), bf16[2,12,1]{1,2,0:T(2,128)(2,1)S(1)}, u32[]{:S(2)}, u32[]{:S(2)}) async-start(bf16[2,12,1]{1,2,0:T(2,128)(2,1)} %all_to_all.71), calls=%async_computation.3 | async-start | bytes 2048 | tf_op jit(solution)/shard_map/all_to_all | solution.py:66
  13.8 1.1 convolution_convert_fusion.3
  14.9 0.8 all_to_all.62
  15.7 1.8 all-to-all-done.2
  17.5 3.4 %all-to-all-start.3 = ((bf16[2,12,4096]{2,1,0:T(8,128)(2,1)}), bf16[2,12,4096]{2,1,0:T(8,128)(2,1)S(1)}, u32[]{:S(2)}, u32[]{:S(2)}) async-start(bf16[2,12,4096]{2,1,0:T(8,128)(2,1)} %all_to_all.62), calls=%async_computation.4 | async-start | bytes 524288 | tf_op jit(solution)/shard_map/all_to_all | solution.py:64
  21.0 0.0 copy-done.2
  21.0 0.7 copy.30
  21.7 4.5 %all-to-all-done.3 = bf16[2,12,4096]{2,1,0:T(8,128)(2,1)S(1)} async-done(((bf16[2,12,4096]{2,1,0:T(8,128)(2,1)}), bf16[2,12,4096]{2,1,0:T(8,128)(2,1)S(1)}, u32[]{:S(2)}, u32[]{:S(2)}) %all-to-all-start.3) | async-done | bytes 196640 | tf_op jit(solution)/shard_map/all_to_all | solution.py:64
  26.1 3.4 %all-to-all-start = ((bf16[24,4,1024]{2,0,1:T(8,128)(2,1)}), bf16[24,4,1024]{2,0,1:T(8,128)(2,1)S(1)}, u32[]{:S(2)}, u32[]{:S(2)}) async-start(bf16[24,4,1024]{2,0,1:T(8,128)(2,1)} %bitcast.43), calls=%async_computation | async-start | bytes 393216 | tf_op jit(solution)/shard_map/all_to_all | solution.py:29
  29.5 0.0 copy-done
  29.5 0.3 convolution_convert_fusion
  29.8 1.1 all_to_all.68
  30.9 0.0 copy-start.3
  30.9 3.8 %all-to-all-done = bf16[24,4,1024]{2,0,1:T(8,128)(2,1)S(1)} async-done(((bf16[24,4,1024]{2,0,1:T(8,128)(2,1)}), bf16[24,4,1024]{2,0,1:T(8,128)(2,1)S(1)}, u32[]{:S(2)}, u32[]{:S(2)}) %all-to-all-start) | async-done | bytes 196640 | tf_op jit(solution)/shard_map/all_to_all | solution.py:29
  34.8 3.6 %all-to-all-start.5 = ((bf16[2,12,14336]{2,1,0:T(8,128)(2,1)}), bf16[2,12,14336]{2,1,0:T(8,128)(2,1)S(1)}, u32[]{:S(2)}, u32[]{:S(2)}) async-start(bf16[2,12,14336]{2,1,0:T(8,128)(2,1)} %all_to_all.68), calls=%async_computation.6 | async-start | bytes 1835008 | tf_op jit(solution)/shard_map/all_to_all | solution.py:65
  38.3 0.0 all-reduce.4.cloned.1.call-start
  38.4 0.1 eq.45
  38.5 0.1 all_to_all.64
  38.5 0.0 copy-done.3
  38.6 0.2 fusion.2
  38.7 15.7 %all_gather.3 = bf16[192,1024]{1,0:T(8,128)(2,1)S(1)} all-gather(bf16[96,1024]{1,0:T(8,128)(2,1)S(1)} %bitcast.47), channel_id=1, replica_groups=mesh['dp'=4,'adapter'=2,'fsdp'=4] {'adapter'}, dimensions={0}, use_global_device_ids=true | all-gather | bytes 589824 | tf_op jit(solution)/shard_map/all_gather | solution.py:30
  54.5 0.0 copy-start.1
  54.5 0.0 all-to-all-done.5
  54.5 0.2 all_to_all.70
  54.7 1.1 convolution_convert_fusion.1
  55.8 0.0 all-reduce.4.cloned.1.call-update
  55.8 0.0 all-reduce.8.cloned.1.call-start
  55.8 0.0 copy-done.1
  55.8 1.2 convolution_convert_fusion.4
  57.1 0.0 all-reduce.8.cloned.1.call-update
  57.1 0.0 reduce-scatter.2.cloned.1.call-start
  57.1 11.8 %convolution_convert_fusion.2 = bf16[192,7168]{1,0:T(8,128)(2,1)} fusion(bf16[192,1024]{1,0:T(8,128)(2,1)S(1)} %bitcast.49, bf16[7168,1024]{1,0:T(8,128)(2,1)} %param.9), kind=kOutput, calls=%fused_computation.6 | convolution fusion | flops 2819948544 | bytes 17825792 | tf_op jit(solution)/shard_map/dot_general | solution.py:38
  68.9 0.0 reduce-scatter.2.cloned.1.call-update
  68.9 0.4 fusion
  69.3 1.1 all_to_all.65
  70.4 3.6 %all-to-all-start.4 = ((bf16[2,12,14336]{2,1,0:T(8,128)(2,1)}), bf16[2,12,14336]{2,1,0:T(8,128)(2,1)S(1)}, u32[]{:S(2)}, u32[]{:S(2)}) async-start(bf16[2,12,14336]{2,1,0:T(8,128)(2,1)} %all_to_all.65), calls=%async_computation.5 | async-start | bytes 1835008 | tf_op jit(solution)/shard_map/all_to_all | solution.py:106
  74.0 0.0 all-reduce.6.cloned.1.call-start
  74.0 15.2 %all-reduce.4.cloned.1.call-done = bf16[16,14336]{1,0:T(8,128)(2,1)} async-done(((bf16[16,14336]{1,0:T(8,128)(2,1)}), bf16[16,14336]{1,0:T(8,128)(2,1)}) %all-reduce.4.cloned.1.call-update) | async-done | bytes 458768 | tf_op jit(solution)/shard_map/psum | solution.py:114
  89.2 0.0 all-reduce.6.cloned.1.call-update
  89.3 92.2 %all-reduce.8.cloned.1.call-done = bf16[16,4096]{1,0:T(8,128)(2,1)} async-done(((bf16[16,4096]{1,0:T(8,128)(2,1)}), bf16[16,4096]{1,0:T(8,128)(2,1)}) %all-reduce.8.cloned.1.call-update) | async-done | bytes 131088 | tf_op jit(solution)/shard_map/psum | solution.py:115
  181.5 1.6 multiply_bitcast_fusion.1
  183.1 0.0 all-to-all-done.4
  183.1 0.2 all_to_all.67
  183.3 37.7 %reduce-scatter.2.cloned.1.call-done = bf16[48,7168]{1,0:T(8,128)(2,1)} async-done(((bf16[192,7168]{1,0:T(8,128)(2,1)}), bf16[48,7168]{1,0:T(8,128)(2,1)}) %reduce-scatter.2.cloned.1.call-update) | async-done | bytes 688144 | tf_op jit(solution)/shard_map/reduce_scatter | solution.py:37
  221.0 3.5 %all-to-all-start.1 = ((bf16[2,24,7168]{2,1,0:T(8,128)(2,1)}), bf16[2,24,7168]{2,1,0:T(8,128)(2,1)S(1)}, u32[]{:S(2)}, u32[]{:S(2)}) async-start(bf16[2,24,7168]{2,1,0:T(8,128)(2,1)} %bitcast.48), calls=%async_computation.2 | async-start | bytes 1376256 | tf_op jit(solution)/shard_map/all_to_all | solution.py:45
  224.5 36.3 %all-reduce.6.cloned.1.call-done = bf16[16,14336]{1,0:T(8,128)(2,1)} async-done(((bf16[16,14336]{1,0:T(8,128)(2,1)}), bf16[16,14336]{1,0:T(8,128)(2,1)}) %all-reduce.6.cloned.1.call-update) | async-done | bytes 458768 | tf_op jit(solution)/shard_map/psum | solution.py:114
  260.8 2.0 multiply_bitcast_fusion
  262.8 0.0 all-to-all-done.1
  262.8 0.1 convert_bitcast_fusion
  262.9 0.1 copy.28
  263.0 1.2 fusion.1
  (2 shorter events, 0.0 us)
Async XLA Ops:
  7.2 22.3 %copy-start = (bf16[24,14336]{1,0:T(8,128)(2,1)S(1)}, bf16[24,14336]{1,0:T(8,128)(2,1)}, u32[]{:S(2)}) copy-start(bf16[24,14336]{1,0:T(8,128)(2,1)} %param.8) | copy-start | bytes 2064388
  7.2 13.8 %copy-start.2 = (bf16[24,4096]{1,0:T(8,128)(2,1)S(1)}, bf16[24,4096]{1,0:T(8,128)(2,1)}, u32[]{:S(2)}) copy-start(bf16[24,4096]{1,0:T(8,128)(2,1)} %param.7) | copy-start | bytes 589828
  9.6 7.9 %all-to-all-start.2 = ((bf16[2,12,1]{1,2,0:T(2,128)(2,1)}), bf16[2,12,1]{1,2,0:T(2,128)(2,1)S(1)}, u32[]{:S(2)}, u32[]{:S(2)}) async-start(bf16[2,12,1]{1,2,0:T(2,128)(2,1)} %all_to_all.71), calls=%async_computation.3 | async-start | bytes 2048 | tf_op jit(solution)/shard_map/all_to_all | solution.py:66
  17.5 8.6 %all-to-all-start.3 = ((bf16[2,12,4096]{2,1,0:T(8,128)(2,1)}), bf16[2,12,4096]{2,1,0:T(8,128)(2,1)S(1)}, u32[]{:S(2)}, u32[]{:S(2)}) async-start(bf16[2,12,4096]{2,1,0:T(8,128)(2,1)} %all_to_all.62), calls=%async_computation.4 | async-start | bytes 524288 | tf_op jit(solution)/shard_map/all_to_all | solution.py:64
  26.1 8.6 %all-to-all-start = ((bf16[24,4,1024]{2,0,1:T(8,128)(2,1)}), bf16[24,4,1024]{2,0,1:T(8,128)(2,1)S(1)}, u32[]{:S(2)}, u32[]{:S(2)}) async-start(bf16[24,4,1024]{2,0,1:T(8,128)(2,1)} %bitcast.43), calls=%async_computation | async-start | bytes 393216 | tf_op jit(solution)/shard_map/all_to_all | solution.py:29
  30.9 7.6 %copy-start.3 = (bf16[1,16,4096]{2,1,0:T(8,128)(2,1)S(1)}, bf16[1,16,4096]{2,1,0:T(8,128)(2,1)}, u32[]{:S(2)}) copy-start(bf16[1,16,4096]{2,1,0:T(8,128)(2,1)} %param.11) | copy-start | bytes 393220
  34.8 19.7 %all-to-all-start.5 = ((bf16[2,12,14336]{2,1,0:T(8,128)(2,1)}), bf16[2,12,14336]{2,1,0:T(8,128)(2,1)S(1)}, u32[]{:S(2)}, u32[]{:S(2)}) async-start(bf16[2,12,14336]{2,1,0:T(8,128)(2,1)} %all_to_all.68), calls=%async_computation.6 | async-start | bytes 1835008 | tf_op jit(solution)/shard_map/all_to_all | solution.py:65
  38.3 50.9 %all-reduce.4.cloned.1.call-start = ((), (), s32[]{:S(2)}) async-start(), calls=%async_computation.8 | async-start | bytes 917504 | tf_op jit(solution)/shard_map/psum | solution.py:114
  54.5 1.4 copy-start.1
  55.8 125.7 %all-reduce.8.cloned.1.call-start = ((), (), s32[]{:S(2)}) async-start(), calls=%async_computation.10 | async-start | bytes 262144 | tf_op jit(solution)/shard_map/psum | solution.py:115
  57.1 163.9 %reduce-scatter.2.cloned.1.call-start = ((), (), s32[]{:S(2)}) async-start(), calls=%async_computation.7 | async-start | bytes 3440640 | tf_op jit(solution)/shard_map/reduce_scatter | solution.py:37
  70.4 112.7 %all-to-all-start.4 = ((bf16[2,12,14336]{2,1,0:T(8,128)(2,1)}), bf16[2,12,14336]{2,1,0:T(8,128)(2,1)S(1)}, u32[]{:S(2)}, u32[]{:S(2)}) async-start(bf16[2,12,14336]{2,1,0:T(8,128)(2,1)} %all_to_all.65), calls=%async_computation.5 | async-start | bytes 1835008 | tf_op jit(solution)/shard_map/all_to_all | solution.py:106
  74.0 186.8 %all-reduce.6.cloned.1.call-start = ((), (), s32[]{:S(2)}) async-start(), calls=%async_computation.9 | async-start | bytes 917504 | tf_op jit(solution)/shard_map/psum | solution.py:114
  221.0 41.8 %all-to-all-start.1 = ((bf16[2,24,7168]{2,1,0:T(8,128)(2,1)}), bf16[2,24,7168]{2,1,0:T(8,128)(2,1)S(1)}, u32[]{:S(2)}, u32[]{:S(2)}) async-start(bf16[2,24,7168]{2,1,0:T(8,128)(2,1)} %bitcast.48), calls=%async_computation.2 | async-start | bytes 1376256 | tf_op jit(solution)/shard_map/all_to_all | solution.py:45
Sparse Core Ops, SparseCore 0:
  55.9 33.2 all-reduce.3
  93.3 88.1 all-reduce.7
  184.1 36.8 reduce-scatter.1
  223.2 37.5 all-reduce.5
